TPU v7x, 32 devices: a whole 2x2x4 slice. The times are simulated.
32 devices in a mesh: row: 2 (over core), pitch: 4 (over y, x), span: 4 (over z).
Axes of the slice: x: 2, y: 2, z: 4, core: 2. Of those that a mesh axis runs over, the one named last changes fastest.
Arguments:
- snapshots: bfloat16 [2, 20, 3, 32, 256, 256], P('row', None, None, 'pitch', 'span'), may hold values from -6 to 6
- snap_index: int32 [16], replicated, may hold values from 0 to 19, as said below
- flow_state: float32 [2, 5, 32, 256, 256], P('row', None, 'pitch', 'span'), may hold values from -6 to 6
- eddy_viscosity: float32 [2, 32, 256, 256], P('row', 'pitch', 'span'), may hold values from 0.04 to 0.4
- intersection: int32 [2, 32], P('row'), may hold values from 0 to 31, as said below
- counts: int32 [2, 32], P('row'), may hold values from 1 to 8, as said below
Outputs:
- received_stress: float32 [2, 6, 256, 256], P('row', None, 'span')
- new_state: float32 [2, 5, 32, 256, 256], P('row', None, 'pitch', 'span')
Inputs may be any that keep to these rules, and one draw needn't show every extreme that they name: `snap_index`: 16 distinct slots, among them slot 0 and slot 19. `intersection`: for each row, a one-to-one map of blocks. Call blocks k * 8 to (k + 1) * 8 - 1 group k: the blocks of one group take their sources from at most 2 blocks of any one group of the other layout, and exactly 2 for some pairs of groups. `counts`: each row has a block with all 8 cells live.
All inputs are finite; a program needn't handle non-finite values.
Results may differ from a plain program's by a relative error of at most 0.0003.
Values sent between devices are 32-bit elements; how exact they have to be, the bound alone decides.
A program may use at most 128 MiB of HBM per device.

v0:
```python
import jax
import jax.numpy as jnp
from jax import lax
from jax.sharding import PartitionSpec as P

SNAPS = 16
BLOCK = 8
CAPACITY = 2


stress_pairs = ((0, 0), (0, 1), (0, 2), (1, 1), (1, 2), (2, 2))
time_step = 0.1


def padded_2(block, sides, width, periodic):
    for axis, dim in sides:
        count = lax.axis_size(axis)
        forward = [(i, i + 1) for i in range(count - 1)]
        if periodic:
            forward.append((count - 1, 0))
        backward = [(target, source) for source, target in forward]
        low = lax.ppermute(
            lax.slice_in_dim(block, block.shape[dim] - width, None, axis=dim), axis, forward
        )
        high = lax.ppermute(lax.slice_in_dim(block, 0, width, axis=dim), axis, backward)
        block = jnp.concatenate([low, block, high], axis=dim)
    return block


def partner(block, axis, bit):
    count = lax.axis_size(axis)
    route = []
    for low in range(count):
        high = low | 1 << bit
        if high != low and high < count:
            route += [(low, high), (high, low)]
    return lax.ppermute(block, axis, route)


def axial_diff(values):
    padded = jnp.concatenate([values[..., :1], values, values[..., -1:]], axis=-1)
    return (padded[..., 2:] - padded[..., :-2]) * 0.5


def residual(flow_field, speed, viscosity, live_mask, forcing):
    around_pitch = padded_2(flow_field, (("pitch", 1),), 1, True)
    around_span = padded_2(flow_field, (("span", 2),), 1, False)
    axial_pad = jnp.concatenate([flow_field[..., :1], flow_field, flow_field[..., -1:]], axis=3)
    laplace = (
        around_pitch[:, 2:]
        + around_pitch[:, :-2]
        + around_span[:, :, 2:]
        + around_span[:, :, :-2]
        + axial_pad[..., 2:]
        + axial_pad[..., :-2]
        - 6.0 * flow_field
    )
    return live_mask * (-axial_diff(speed * flow_field) + viscosity * laplace + forcing)


def deliver(values, block_links):
    swapped = partner(values, "row", 0)
    span_count = lax.axis_size("span")
    blocks_all = block_links.shape[0]
    per_dev = blocks_all // span_count
    share_len = swapped.shape[2]
    block_len = swapped.shape[1] // per_dev
    position = lax.axis_index("span")
    block_ids = jnp.arange(blocks_all, dtype=jnp.int32)
    pairing = (block_links[:, None] == block_ids[None, :]).astype(jnp.int32)
    target = jnp.sum(pairing * block_ids[:, None], axis=0)
    target_dev = target // per_dev
    source_dev = block_ids // per_dev
    earlier = (
        (source_dev[:, None] == source_dev[None, :])
        & (target_dev[:, None] == target_dev[None, :])
        & (block_ids[None, :] < block_ids[:, None])
    )
    slot_of = jnp.sum(earlier.astype(jnp.int32), axis=1)
    devices = jnp.arange(span_count, dtype=jnp.int32)
    places = jnp.arange(CAPACITY, dtype=jnp.int32)
    my_dev = lax.dynamic_slice_in_dim(target_dev, position * per_dev, per_dev)
    my_slot = lax.dynamic_slice_in_dim(slot_of, position * per_dev, per_dev)
    placing = (
        (my_dev[:, None, None] == devices[None, :, None])
        & (my_slot[:, None, None] == places[None, None, :])
    ).astype(jnp.float32)
    blocks = swapped.reshape(6, per_dev, block_len * share_len)
    outgoing = jnp.einsum("jnc,mjw->ncmw", placing, blocks, precision=lax.Precision.HIGHEST)
    incoming = lax.all_to_all(outgoing, "span", split_axis=0, concat_axis=0, tiled=True)
    wanted = lax.dynamic_slice_in_dim(block_links, position * per_dev, per_dev)
    from_dev = wanted // per_dev
    from_slot = jnp.sum(
        (wanted[:, None] == block_ids[None, :]).astype(jnp.int32) * slot_of[None, :], axis=1
    )
    choosing = (
        (from_dev[:, None, None] == devices[None, :, None])
        & (from_slot[:, None, None] == places[None, None, :])
    ).astype(jnp.float32)
    arrived = jnp.einsum("knc,ncmw->mkw", choosing, incoming, precision=lax.Precision.HIGHEST)
    return arrived.reshape(6, per_dev * block_len, share_len)


def body(snapshots, snap_index, flow_state, eddy_viscosity, intersection, counts):
    stored = snapshots[0]
    start = flow_state[0]
    viscosity = eddy_viscosity[0]
    block_links = intersection[0]
    block_counts = counts[0]
    pitch_cells = stored.shape[2]
    span_cells = stored.shape[3]
    axial_cells = stored.shape[4]
    pitch_total = pitch_cells * lax.axis_size("pitch")

    def select_slot(slot):
        return lax.dynamic_index_in_dim(stored, slot, 0, keepdims=False).astype(jnp.float32)

    def add_mean(step_num, running):
        return running + select_slot(snap_index[step_num])

    running = lax.fori_loop(0, SNAPS, add_mean, jnp.zeros(stored.shape[1:], jnp.float32))
    time_mean = running / SNAPS

    def add_products(step_num, running):
        fluct = select_slot(snap_index[step_num]) - time_mean
        return running + jnp.stack([jnp.sum(fluct[p] * fluct[q], axis=0) for p, q in stress_pairs])

    summed = lax.fori_loop(
        0, SNAPS, add_products, jnp.zeros((6, span_cells, axial_cells), jnp.float32)
    )
    partial_value = summed / (SNAPS * pitch_total)
    totals = lax.psum(partial_value, "pitch")
    received = deliver(totals, block_links)
    position = lax.axis_index("span")
    span_total = span_cells * lax.axis_size("span")
    span_pos = (
        (position * span_cells + jnp.arange(span_cells, dtype=jnp.int32)).astype(jnp.float32) + 0.5
    ) / span_total
    curvature = (1.0 / (1.0 + span_pos))[:, None]
    source_x = -axial_diff(received[0]) - curvature * received[1]
    source_r = -axial_diff(received[1]) + curvature * (received[5] - received[3])
    source_t = -axial_diff(received[2]) - 2.0 * curvature * received[4]
    energy = time_mean[0] * source_x + time_mean[1] * source_r + time_mean[2] * source_t
    forcing = jnp.concatenate(
        [
            jnp.zeros((1, pitch_cells, span_cells, axial_cells), jnp.float32),
            jnp.broadcast_to(
                jnp.stack([source_x, source_r, source_t])[:, None],
                (3, pitch_cells, span_cells, axial_cells),
            ),
            energy[None],
        ],
        axis=0,
    )
    per_dev = span_cells // BLOCK
    my_counts = lax.dynamic_slice_in_dim(block_counts, position * per_dev, per_dev)
    live_mask = (jnp.arange(BLOCK, dtype=jnp.int32)[None, :] < my_counts[:, None]).astype(
        jnp.float32
    )
    live_mask = live_mask.reshape(span_cells)[:, None]
    speed = 0.5 + time_mean[0]
    section_one = start + time_step * residual(start, speed, viscosity, live_mask, forcing)
    finished = 0.5 * (
        start
        + section_one
        + time_step * residual(section_one, speed, viscosity, live_mask, forcing)
    )
    return (received[None], finished[None])


def solution(mesh):
    return jax.shard_map(
        body,
        mesh=mesh,
        in_specs=(
            P("row", None, None, "pitch", "span", None),
            P(),
            P("row", None, "pitch", "span", None),
            P("row", "pitch", "span", None),
            P("row", None),
            P("row", None),
        ),
        out_specs=(P("row", None, "span", None), P("row", None, "pitch", "span", None)),
        check_vma=False,
    )
```

profile of v0, /device:TPU:0, one launch (start us, length us, event | category | flops | bytes accessed | tf_op | source)
XLA Modules:
  0.0 288.5 jit_solution(12164644477243232642)
XLA Ops:
  7.2 1.8 fusion.64
  10.3 6.2 %collective-permute-start.4 = (f32[5,8,1,256]{3,2,1,0:T(1,128)}, f32[5,8,1,256]{3,2,1,0:T(1,128)}, u32[]{:S(2)}, u32[]{:S(2)}) collective-permute-start(f32[5,8,1,256]{3,2,1,0:T(1,128)} %get-tuple-element.251), channel_id=1, source_target_pairs={{0,1},{1,2},{2,3},{4,5},{5,6},{6,7},{8,9},{9,10},{10,11},{12,13},{... | collective-permute-start | bytes 122888 | tf_op jit(solution)/shard_map/ppermute | solution.py:22
  16.5 2.0 fusion.63
  18.4 2.9 collective-permute-start.1
  21.3 77.6 %while.28 = (s32[]{:T(128)}, f32[3,8,64,256]{3,2,1,0:T(8,128)S(1)}, s32[16]{0:T(128)}, bf16[20,3,8,64,256]{4,3,2,1,0:T(8,128)(2,1)}, s32[]{:T(128)}, /*index=5*/s32[]{:T(128)}, s32[]{:T(128)}) while((s32[]{:T(128)}, f32[3,8,64,256]{3,2,1,0:T(8,128)S(1)}, s32[16]{0:T(128)}, bf16[20,3,8,64,256]{4,3,2,1,0:T(8,128)(2,1)}, s32[]{:T(128)}, ...), condition=%wide.region_3.0_spmd.clone, body=%wide.region_2.3_spmd.clone.sunk | while | flops 1179654 | bytes 3932305 | solution.py:121
  24.5 1.7 convert_add_fusion.2
  39.0 1.7 convert_add_fusion.2
  43.9 1.7 convert_add_fusion.2
  48.7 1.7 convert_add_fusion.2
  53.6 1.7 convert_add_fusion.2
  99.6 69.6 %while.29 = (s32[]{:T(128)}, f32[6,64,256]{2,1,0:T(8,128)S(1)}, s32[16]{0:T(128)S(1)}, bf16[20,3,8,64,256]{4,3,2,1,0:T(8,128)(2,1)}, f32[3,8,64,256]{3,2,1,0:T(8,128)S(1)}, /*index=5*/s32[]{:T(128)}, s32[]{:T(128)}, s32[]{:T(128)}) while((s32[]{:T(128)}, f32[6,64,256]{2,1,0:T(8,128)S(1)}, s32[16]{0:T(128)S(1)}, ...), condition=%wide.region_11.12_spmd.clone, body=%wide.region_4.11_spmd.clone.sunk | while | flops 2457606 | bytes 7864473 | solution.py:128
  170.7 44.2 %all-reduce.2.cloned.1.call-done = f32[6,64,256]{2,1,0:T(8,128)} async-done(((f32[6,64,256]{2,1,0:T(8,128)}), f32[6,64,256]{2,1,0:T(8,128)}) %all-reduce.2.cloned.1.call-update) | async-done | bytes 393232 | tf_op jit(solution)/shard_map/psum | solution.py:132
  215.0 1.9 collective-permute-done
  218.2 4.6 %all-to-all-start = ((f32[4,2,6,2048]{3,1,2,0:T(2,128)}), f32[4,2,6,2048]{3,1,2,0:T(2,128)S(1)}, u32[]{:S(2)}, u32[]{:S(2)}) async-start(f32[4,2,6,2048]{3,1,2,0:T(2,128)} %fusion.48), calls=%async_computation | async-start | bytes 786432 | tf_op jit(solution)/shard_map/all_to_all | solution.py:90
  222.9 3.2 %fusion.65 = (f32[5,8,64,1]{3,2,1,0:T(8,128)S(1)}, f32[5,8,64,1]{3,2,1,0:T(8,128)}) fusion(f32[5,8,64,256]{3,2,1,0:T(8,128)} %bitcast.77), kind=kLoop, calls=%fused_computation.139 | loop fusion | bytes 40960 | tf_op jit(solution)/shard_map/slice | solution.py:48
  226.1 8.6 %all-to-all-done = f32[4,2,6,2048]{3,1,2,0:T(2,128)S(1)} async-done(((f32[4,2,6,2048]{3,1,2,0:T(2,128)}), f32[4,2,6,2048]{3,1,2,0:T(2,128)S(1)}, u32[]{:S(2)}, u32[]{:S(2)}) %all-to-all-start) | async-done | bytes 393248 | tf_op jit(solution)/shard_map/all_to_all | solution.py:90
  238.3 2.0 fusion.62
  240.5 6.7 %broadcast_multiply_fusion = (f32[5,8,64,256]{3,2,1,0:T(8,128)S(1)}, f32[5,8,64,256]{3,2,1,0:T(8,128)S(1)}) fusion(f32[8,64,256]{2,1,0:T(8,128)S(1)} %get-tuple-element.255, f32[5,8,64,256]{3,2,1,0:T(8,128)S(1)} %bitcast.78, f32[1,8,64,256]{3,2,1,0:T(8,128)S(1)} %get-tuple-element.254, f32[3,8,64,256]{3,2,1,0:T(8,128)S(1)} %broadcast_in_dim.13, ...), kind=kLoop, calls=%fused_computation.65 | loop fusion | flops 17694720 | bytes 14410004 | tf_op jit(solution)/shard_map/mul | solution.py:58
  248.3 1.9 fusion.61
  254.2 4.5 %collective-permute-start.8 = (f32[5,8,1,256]{3,2,1,0:T(1,128)S(1)}, f32[5,8,1,256]{3,2,1,0:T(1,128)S(1)}, u32[]{:S(2)}, u32[]{:S(2)}) collective-permute-start(f32[5,8,1,256]{3,2,1,0:T(1,128)S(1)} %get-tuple-element.243), channel_id=1, source_target_pairs={{0,1},{1,2},{2,3},{4,5},{5,6},{6,7},{8,9},{9,10},{10,11},{12,13},{... | collective-permute-start | bytes 122888 | tf_op jit(solution)/shard_map/ppermute | solution.py:22
  258.7 1.9 fusion.58
  260.7 1.8 broadcast_in_dim_reshape.3
  262.5 4.6 %collective-permute-done.6 = f32[5,1,64,256]{3,2,1,0:T(8,128)} collective-permute-done((f32[5,1,64,256]{3,2,1,0:T(8,128)}, f32[5,1,64,256]{3,2,1,0:T(8,128)}, u32[]{:S(2)}, u32[]{:S(2)}) %collective-permute-start.6) | collective-permute-done | bytes 327712 | tf_op jit(solution)/shard_map/ppermute | solution.py:22
  267.0 14.6 %fusion.9 = f32[1,5,8,64,256]{4,3,2,1,0:T(8,128)} fusion(f32[5,8,64,256]{3,2,1,0:T(8,128)} %copy-done.2, f32[5,8,64,1]{3,2,1,0:T(8,128)} %get-tuple-element.245, f32[5,8,64,1]{3,2,1,0:T(8,128)S(1)} %get-tuple-element.244, f32[5,8,1,256]{3,2,1,0:T(1,128)S(1)} %collective-permute-done.8, f32[5,8,1,256]{3,2,1,0:T(1,128)S(1)} %collective-permute-done.7, ...), kind=kLoop, calls=%fused_computation.25 | loop fusion | flops 18350080 | bytes 13885716 | tf_op jit(solution)/shard_map/broadcast_in_dim | solution.py:168
  (256 shorter events, 89.3 us)
Async XLA Ops:
  7.2 162.8 %copy-start = (s32[1,32]{1,0:T(1,128)S(1)}, s32[1,32]{1,0:T(1,128)}, u32[]{:S(2)}) copy-start(s32[1,32]{1,0:T(1,128)} %param.15) | copy-start | bytes 388
  7.2 207.7 %all-reduce.2.cloned.1.call-start = ((), (), s32[]{:S(2)}) async-start(), calls=%async_computation.1 | async-start | bytes 786432 | tf_op jit(solution)/shard_map/psum | solution.py:132
  9.0 231.3 %collective-permute-start.3 = (f32[5,8,1,256]{3,2,1,0:T(1,128)}, f32[5,8,1,256]{3,2,1,0:T(1,128)}, u32[]{:S(2)}, u32[]{:S(2)}) collective-permute-start(f32[5,8,1,256]{3,2,1,0:T(1,128)} %get-tuple-element.250), channel_id=1, source_target_pairs={{1,0},{2,1},{3,2},{5,4},{6,5},{7,6},{9,8},{10,9},{11,10},{13,12},{... | collective-permute-start | bytes 122888 | tf_op jit(solution)/shard_map/ppermute | solution.py:25
  10.3 230.1 %collective-permute-start.4 = (f32[5,8,1,256]{3,2,1,0:T(1,128)}, f32[5,8,1,256]{3,2,1,0:T(1,128)}, u32[]{:S(2)}, u32[]{:S(2)}) collective-permute-start(f32[5,8,1,256]{3,2,1,0:T(1,128)} %get-tuple-element.251), channel_id=1, source_target_pairs={{0,1},{1,2},{2,3},{4,5},{5,6},{6,7},{8,9},{9,10},{10,11},{12,13},{... | collective-permute-start | bytes 122888 | tf_op jit(solution)/shard_map/ppermute | solution.py:22
  18.4 221.9 %collective-permute-start.1 = (f32[5,1,64,256]{3,2,1,0:T(8,128)}, f32[5,1,64,256]{3,2,1,0:T(8,128)}, u32[]{:S(2)}, u32[]{:S(2)}) collective-permute-start(f32[5,1,64,256]{3,2,1,0:T(8,128)} %get-tuple-element.248), channel_id=1, source_target_pairs={{4,0},{8,4},{12,8},{0,12},{5,1},{9,5},{13,9},{1,13},{6,2},{10,6},{... | collective-permute-start | bytes 983048 | tf_op jit(solution)/shard_map/ppermute | solution.py:25
  21.3 219.0 %collective-permute-start.2 = (f32[5,1,64,256]{3,2,1,0:T(8,128)}, f32[5,1,64,256]{3,2,1,0:T(8,128)}, u32[]{:S(2)}, u32[]{:S(2)}) collective-permute-start(f32[5,1,64,256]{3,2,1,0:T(8,128)} %get-tuple-element.249), channel_id=1, source_target_pairs={{0,4},{4,8},{8,12},{12,0},{1,5},{5,9},{9,13},{13,1},{2,6},{6,10},{... | collective-permute-start | bytes 983048 | tf_op jit(solution)/shard_map/ppermute | solution.py:22
  98.9 0.7 copy-start.6
  99.5 70.5 %copy-start.5 = (s32[1,32]{1,0:T(1,128)S(1)}, s32[1,32]{1,0:T(1,128)}, u32[]{:S(2)}) copy-start(s32[1,32]{1,0:T(1,128)} %param.14) | copy-start | bytes 388
  214.9 1.9 collective-permute-start
  218.2 16.6 %all-to-all-start = ((f32[4,2,6,2048]{3,1,2,0:T(2,128)}), f32[4,2,6,2048]{3,1,2,0:T(2,128)S(1)}, u32[]{:S(2)}, u32[]{:S(2)}) async-start(f32[4,2,6,2048]{3,1,2,0:T(2,128)} %fusion.48), calls=%async_computation | async-start | bytes 786432 | tf_op jit(solution)/shard_map/all_to_all | solution.py:90
  235.3 0.8 copy-start.4
  236.3 1.7 copy-start.1
  247.3 4.9 %copy-start.2 = (f32[5,8,64,256]{3,2,1,0:T(8,128)}, f32[5,8,64,256]{3,2,1,0:T(8,128)S(1)}, u32[]{:S(2)}) copy-start(f32[5,8,64,256]{3,2,1,0:T(8,128)S(1)} %get-tuple-element.235) | copy-start | bytes 7864324
  247.3 11.5 %copy-start.3 = (f32[5,8,64,256]{3,2,1,0:T(8,128)}, f32[5,8,64,256]{3,2,1,0:T(8,128)S(1)}, u32[]{:S(2)}) copy-start(f32[5,8,64,256]{3,2,1,0:T(8,128)S(1)} %get-tuple-element.234) | copy-start | bytes 7864324
  250.2 12.3 %collective-permute-start.5 = (f32[5,1,64,256]{3,2,1,0:T(8,128)}, f32[5,1,64,256]{3,2,1,0:T(8,128)}, u32[]{:S(2)}, u32[]{:S(2)}) collective-permute-start(f32[5,1,64,256]{3,2,1,0:T(8,128)} %get-tuple-element.240), channel_id=1, source_target_pairs={{4,0},{8,4},{12,8},{0,12},{5,1},{9,5},{13,9},{1,13},{6,2},{10,6},{... | collective-permute-start | bytes 983048 | tf_op jit(solution)/shard_map/ppermute | solution.py:25
  251.6 15.4 %collective-permute-start.6 = (f32[5,1,64,256]{3,2,1,0:T(8,128)}, f32[5,1,64,256]{3,2,1,0:T(8,128)}, u32[]{:S(2)}, u32[]{:S(2)}) collective-permute-start(f32[5,1,64,256]{3,2,1,0:T(8,128)} %get-tuple-element.241), channel_id=1, source_target_pairs={{0,4},{4,8},{8,12},{12,0},{1,5},{5,9},{9,13},{13,1},{2,6},{6,10},{... | collective-permute-start | bytes 983048 | tf_op jit(solution)/shard_map/ppermute | solution.py:22
  252.9 9.6 %collective-permute-start.7 = (f32[5,8,1,256]{3,2,1,0:T(1,128)}, f32[5,8,1,256]{3,2,1,0:T(1,128)S(1)}, u32[]{:S(2)}, u32[]{:S(2)}) collective-permute-start(f32[5,8,1,256]{3,2,1,0:T(1,128)} %get-tuple-element.242), channel_id=1, source_target_pairs={{1,0},{2,1},{3,2},{5,4},{6,5},{7,6},{9,8},{10,9},{11,10},{13,12},{... | collective-permute-start | bytes 122888 | tf_op jit(solution)/shard_map/ppermute | solution.py:25
  254.2 8.3 %collective-permute-start.8 = (f32[5,8,1,256]{3,2,1,0:T(1,128)S(1)}, f32[5,8,1,256]{3,2,1,0:T(1,128)S(1)}, u32[]{:S(2)}, u32[]{:S(2)}) collective-permute-start(f32[5,8,1,256]{3,2,1,0:T(1,128)S(1)} %get-tuple-element.243), channel_id=1, source_target_pairs={{0,1},{1,2},{2,3},{4,5},{5,6},{6,7},{8,9},{9,10},{10,11},{12,13},{... | collective-permute-start | bytes 122888 | tf_op jit(solution)/shard_map/ppermute | solution.py:22
Sparse Core Ops, SparseCore 0:
  170.0 44.8 all-reduce.1
where the time goes:
time: 291 us; the launch traced here: 289 us
  other arithmetic  77.3 us (27%)
  loops' own time  63.3 us (22%)
  waiting for transfers between devices  59.3 us (20%)
  local copies, waits for them, and re-layouts  49.7 us (17%)
  starting transfers between devices  22.9 us (8%)
  between operations  14.3 us (5%)
    psum x1, waiting for transfers between devices, body(): totals = lax.psum(partial_value, 'pitch')  44.2 us
    another operation x1, loops' own time, body(): lax.fori_loop(0, SNAPS, add_products, jnp.zeros((6, span_cells, axial_cel...  32.4 us
    another operation x1, loops' own time, body(): lax.fori_loop(0, SNAPS, add_mean, jnp.zeros(stored.shape[1:], jnp.float32))  30.9 us
    add x16, other arithmetic, add_mean(): return running + select_slot(snap_index[step_num])  26.5 us
    sub x16, other arithmetic, add_products(): fluct = select_slot(snap_index[step_num]) - time_mean  21.6 us
    dynamic_slice x16, local copies, waits for them, and re-layouts, add_mean(): return running + select_slot(snap_index[step_num])  20.2 us
    broadcast_in_dim x1, other arithmetic, body(): return (received[None], finished[None])  14.6 us
    ppermute x4, starting transfers between devices, padded_2(): lax.ppermute(lax.slice_in_dim(block, block.shape[dim] - width, None, axis...  11.3 us
  transfers between devices with their start and end apart: 11, of which 4 were waited for; matrix products, arithmetic and copies ran while one was open for 35% of the time, Pallas kernels for 0%

commit v1 on v0

v1 whole, which is shorter than its diff:
```python
import functools

import jax
import jax.numpy as jnp
from jax import lax
from jax.experimental import pallas as pl
from jax.experimental.pallas import tpu as pltpu
from jax.sharding import PartitionSpec as P

SNAPS = 16
BLOCK = 8
CAPACITY = 2
LANES = 128
ROWS_BF16 = 16
MESH = pl.DeviceIdType.MESH

stress_pairs = ((0, 0), (0, 1), (0, 2), (1, 1), (1, 2), (2, 2))
time_step = 0.1


def stress_kernel(*refs):
    snaps, (mean_ref, part_ref) = refs[1 : 1 + SNAPS], refs[1 + SNAPS :]
    cells = mean_ref.shape[1]
    halves = mean_ref.shape[3] // LANES
    for h in range(halves):
        cols = slice(h * LANES, (h + 1) * LANES)

        def one(i, acc):
            def load(t):
                return [snaps[t][0, 0, c, i, :, cols].astype(jnp.float32) for c in range(3)]

            base = load(0)
            sums, prods = None, None
            for t in range(1, SNAPS):
                now = load(t)
                d = [now[c] - base[c] for c in range(3)]
                pr = [d[p] * d[q] for p, q in stress_pairs]
                sums = d if sums is None else [a + b for a, b in zip(sums, d)]
                prods = pr if prods is None else [a + b for a, b in zip(prods, pr)]
            shift = [s * (1.0 / SNAPS) for s in sums]
            for c in range(3):
                mean_ref[c, i, :, cols] = base[c] + shift[c]
            return tuple(
                a + (pr - sums[p] * shift[q]) for a, pr, (p, q) in zip(acc, prods, stress_pairs)
            )

        zero = jnp.zeros((ROWS_BF16, LANES), jnp.float32)
        acc = lax.fori_loop(0, cells, one, (zero,) * 6)
        for m in range(6):
            part_ref[m * halves + h] = acc[m]
    for u in range(6 * halves, part_ref.shape[0]):
        part_ref[u] = jnp.zeros((ROWS_BF16, LANES), jnp.float32)


def stresses(snapshots, snap_index, units):
    _, _, comps, pitch, span, axial = snapshots.shape

    def spec(t):
        return pl.BlockSpec(
            (1, 1, comps, pitch, ROWS_BF16, axial), lambda j, idx: (0, idx[t], 0, 0, j, 0)
        )

    return pl.pallas_call(
        stress_kernel,
        out_shape=(
            jax.ShapeDtypeStruct((comps, pitch, span, axial), jnp.float32),
            jax.ShapeDtypeStruct((units, span, LANES), jnp.float32),
        ),
        grid_spec=pltpu.PrefetchScalarGridSpec(
            num_scalar_prefetch=1,
            grid=(span // ROWS_BF16,),
            in_specs=[spec(t) for t in range(SNAPS)],
            out_specs=(
                pl.BlockSpec((comps, pitch, ROWS_BF16, axial), lambda j, idx: (0, 0, j, 0)),
                pl.BlockSpec((units, ROWS_BF16, LANES), lambda j, idx: (0, j, 0)),
            ),
        ),
        cost_estimate=pl.CostEstimate(
            flops=SNAPS * 20 * pitch * span * axial,
            bytes_accessed=SNAPS * comps * pitch * span * axial * 2,
            transcendentals=0,
        ),
    )(snap_index, *([snapshots] * SNAPS))


def next_cell(x):
    lane = lax.broadcasted_iota(jnp.int32, x.shape, 1)
    return jnp.where(lane == x.shape[1] - 1, x, pltpu.roll(x, x.shape[1] - 1, 1))


def last_cell(x):
    lane = lax.broadcasted_iota(jnp.int32, x.shape, 1)
    return jnp.where(lane == 0, x, pltpu.roll(x, 1, 1))


def couple_kernel(
    n_p, n_s, scale,
    links, counts, part, low_face, q_hbm, mean_hbm, visc_hbm,
    rec_out, new_hbm,
    rs_buf, tot, out_buf, a2a, rec, qpad, spad, mean, visc, dtm, src,
    zsend, zrecv,
    rs_s, rs_r, aa_s, aa_r, ag_s, ag_r, hp_s, hp_r, hz_s, hz_r, loc, out_sem,
):
    r, p, s = lax.axis_index("row"), lax.axis_index("pitch"), lax.axis_index("span")
    comps, cells, span, axial = q_hbm.shape
    us = part.shape[0] // n_p
    blocks = span // BLOCK
    halves = axial // LANES
    tile = 16
    top = 8

    load_q = pltpu.make_async_copy(
        q_hbm, qpad.at[:, pl.ds(1, cells), pl.ds(top, span)], loc.at[0]
    )
    load_q.start()
    load_low = pltpu.make_async_copy(low_face, qpad.at[:, 0, pl.ds(top, span)], loc.at[1])
    load_low.start()
    load_mean = pltpu.make_async_copy(mean_hbm, mean, loc.at[2])
    load_mean.start()
    load_visc = pltpu.make_async_copy(visc_hbm, visc, loc.at[3])
    load_visc.start()

    barrier = pltpu.get_barrier_semaphore()
    for d in range(n_p):
        to = lax.rem(p + d, n_p)
        pl.semaphore_signal(barrier, inc=1, device_id=(1 - r, to, s), device_id_type=MESH)
        if d:
            pl.semaphore_signal(barrier, inc=1, device_id=(r, to, s), device_id_type=MESH)
    for d in range(1, n_s):
        to = lax.rem(s + d, n_s)
        pl.semaphore_signal(barrier, inc=1, device_id=(r, p, to), device_id_type=MESH)
    pl.semaphore_wait(barrier, 2 * n_p + n_s - 2)

    scatter = []
    for d in range(n_p):
        to = lax.rem(p + d, n_p)
        scatter.append(pltpu.make_async_remote_copy(
            src_ref=part.at[pl.ds(to * us, us)], dst_ref=rs_buf.at[d],
            send_sem=rs_s.at[d], recv_sem=rs_r.at[d],
            device_id=(1 - r, to, s), device_id_type=MESH,
        ))
    for copy in scatter:
        copy.start()
    right, left = lax.rem(p + 1, n_p), lax.rem(p + n_p - 1, n_p)
    above, below = lax.rem(s + 1, n_s), lax.rem(s + n_s - 1, n_s)
    high_q = pltpu.make_async_remote_copy(
        src_ref=q_hbm.at[:, 0], dst_ref=qpad.at[:, cells + 1, pl.ds(top, span)],
        send_sem=hp_s.at[0], recv_sem=hp_r.at[0],
        device_id=(r, left, s), device_id_type=MESH,
    )
    high_q.start()

    def span_faces(pad, k):
        def pack(i, carry):
            for c in range(comps):
                zsend[k, 0, c, pl.ds(i, 1)] = pad[c, i + 1, top + span - 1 : top + span]
                zsend[k, 1, c, pl.ds(i, 1)] = pad[c, i + 1, top : top + 1]
            return carry

        lax.fori_loop(0, cells, pack, 0)
        copies = []
        for way, to in ((0, above), (1, below)):
            copies.append(pltpu.make_async_remote_copy(
                src_ref=zsend.at[k, way], dst_ref=zrecv.at[k, way],
                send_sem=hz_s.at[k, way], recv_sem=hz_r.at[k, way],
                device_id=(r, p, to), device_id_type=MESH,
            ))
        for copy in copies:
            copy.start()
        return copies

    def span_land(pad, k):
        def land(i, carry):
            for c in range(comps):
                row = zrecv[k, 0, c, pl.ds(i, 1)]
                pad[c, i + 1, top - 1 : top] = jnp.where(s == 0, jnp.zeros_like(row), row)
                row = zrecv[k, 1, c, pl.ds(i, 1)]
                pad[c, i + 1, top + span : top + span + 1] = jnp.where(
                    s == n_s - 1, jnp.zeros_like(row), row
                )
            return carry

        lax.fori_loop(0, cells, land, 0)

    load_q.wait()
    load_low.wait()
    q_span = span_faces(qpad, 0)

    for j in range(span // tile):
        row = lax.broadcasted_iota(jnp.int32, (tile, axial), 0)
        first = counts[s * blocks + 2 * j]
        second = counts[s * blocks + 2 * j + 1]
        limit = jnp.where(row < BLOCK, first, second + BLOCK)
        dtm[j * tile : (j + 1) * tile] = jnp.where(row < limit, time_step, 0.0).astype(jnp.float32)

    for copy in scatter:
        copy.wait()
    for b in range(blocks):
        for u in range(us):
            total = rs_buf[0, u, b * BLOCK : (b + 1) * BLOCK]
            for d in range(1, n_p):
                total = total + rs_buf[d, u, b * BLOCK : (b + 1) * BLOCK]
            tot[u, b] = total * scale

    exchange = []
    for d in range(n_s):
        to = lax.rem(s + d, n_s)
        count = jnp.int32(0)
        picks = [jnp.int32(0)] * CAPACITY
        for k in range(blocks):
            block = links[to * blocks + k]
            here = block // blocks == s
            inside = block % blocks
            for c in range(CAPACITY):
                picks[c] = jnp.where(here & (count == c), inside, picks[c])
            count = count + here.astype(jnp.int32)
        for c in range(CAPACITY):
            for u in range(us):
                if d == 0:
                    a2a[0, c, u] = tot[u, picks[c]]
                else:
                    out_buf[d, c, u] = tot[u, picks[c]]
        if d:
            copy = pltpu.make_async_remote_copy(
                src_ref=out_buf.at[d], dst_ref=a2a.at[d],
                send_sem=aa_s.at[d], recv_sem=aa_r.at[d],
                device_id=(r, p, to), device_id_type=MESH,
            )
            copy.start()
            exchange.append(copy)
    sources = [links[s * blocks + k] // blocks for k in range(blocks)]
    for copy in exchange:
        copy.wait()
    for k in range(blocks):
        slot = jnp.int32(0)
        for e in range(k):
            slot = slot + (sources[e] == sources[k]).astype(jnp.int32)
        slot = jnp.minimum(slot, CAPACITY - 1)
        away = lax.rem(s - sources[k] + n_s, n_s)
        for u in range(us):
            rec[p * us + u, k * BLOCK : (k + 1) * BLOCK] = a2a[away, slot, u]
    gather = []
    for d in range(1, n_p):
        to = lax.rem(p + d, n_p)
        copy = pltpu.make_async_remote_copy(
            src_ref=rec.at[pl.ds(p * us, us)], dst_ref=rec.at[pl.ds(p * us, us)],
            send_sem=ag_s.at[d], recv_sem=ag_r.at[d],
            device_id=(r, to, s), device_id_type=MESH,
        )
        copy.start()
        gather.append(copy)

    for copy in q_span:
        copy.wait()
    span_land(qpad, 0)
    load_mean.wait()
    load_visc.wait()
    high_q.wait()
    for copy in gather:
        copy.wait()

    for j in range(span // tile):
        rows = slice(j * tile, (j + 1) * tile)
        t = [
            jnp.concatenate([rec[m * halves + h, rows] for h in range(halves)], axis=1)
            for m in range(6)
        ]
        for m in range(6):
            rec_out[m, rows] = t[m]
        row = lax.broadcasted_iota(jnp.int32, (tile, axial), 0) + (s * span + j * tile)
        curve = 1.0 / (1.0 + (row.astype(jnp.float32) + 0.5) / (span * n_s))
        diff = [(next_cell(t[m]) - last_cell(t[m])) * 0.5 for m in range(3)]
        live = dtm[rows]
        src[0, rows] = live * (-diff[0] - curve * t[1])
        src[1, rows] = live * (-diff[1] + curve * (t[5] - t[3]))
        src[2, rows] = live * (-diff[2] - 2.0 * curve * t[4])

    def section(pad, i, finish):
        for j in range(span // tile):
            rows = slice(j * tile, (j + 1) * tile)
            nu = visc[i, rows]
            means = [mean[c, i, rows] for c in range(3)]
            speed = 0.5 + means[0]
            live = dtm[rows]
            ahead = live * (nu - 0.5 * next_cell(speed))
            behind = live * (nu + 0.5 * last_cell(speed))
            nu = live * nu
            force = [src[c, rows] for c in range(3)]
            energy = means[0] * force[0] + means[1] * force[1] + means[2] * force[2]
            force = [None] + force + [energy]
            at = top + j * tile
            for c in range(comps):
                x = pad[c, i + 1, at : at + tile]
                around = (
                    pad[c, i, at : at + tile] + pad[c, i + 2, at : at + tile]
                    + pad[c, i + 1, at - 1 : at + tile - 1]
                    + pad[c, i + 1, at + 1 : at + tile + 1]
                )
                step = (
                    ahead * next_cell(x) + behind * last_cell(x) + nu * (around - 6.0 * x)
                )
                if force[c] is not None:
                    step = step + force[c]
                finish(c, i, at, x, step)

    def first(i, carry):
        def finish(c, i, at, x, step):
            spad[c, i + 1, at : at + tile] = x + step

        section(qpad, i, finish)
        return carry

    outs = []

    def second(i, carry):
        def finish(c, i, at, x, step):
            old = qpad[c, i + 1, at : at + tile]
            qpad[c, i + 1, at : at + tile] = 0.5 * (old + x + step)

        section(spad, i, finish)
        return carry

    inner = pl.ds(top, span)
    lax.fori_loop(0, 2, lambda e, carry: first(e * (cells - 1), carry), 0)
    faces = []
    for way, (mine, theirs, to) in enumerate(((cells, 0, right), (1, cells + 1, left))):
        copy = pltpu.make_async_remote_copy(
            src_ref=spad.at[:, mine, inner], dst_ref=spad.at[:, theirs, inner],
            send_sem=hp_s.at[1 + way], recv_sem=hp_r.at[1 + way],
            device_id=(r, to, s), device_id_type=MESH,
        )
        copy.start()
        faces.append(copy)
    lax.fori_loop(1, cells - 1, first, 0)
    s_span = span_faces(spad, 1)
    for copy in s_span:
        copy.wait()
    span_land(spad, 1)
    lax.fori_loop(1, cells - 1, second, 0)
    store_inner = pltpu.make_async_copy(
        qpad.at[:, pl.ds(2, cells - 2), inner], new_hbm.at[:, pl.ds(1, cells - 2)], out_sem.at[0]
    )
    store_inner.start()
    for copy in faces:
        copy.wait()
    lax.fori_loop(0, 2, lambda e, carry: second(e * (cells - 1), carry), 0)
    ends = []
    for e, i in enumerate((0, cells - 1)):
        copy = pltpu.make_async_copy(qpad.at[:, i + 1, inner], new_hbm.at[:, i], out_sem.at[1 + e])
        copy.start()
        ends.append(copy)
    store_inner.wait()
    for copy in ends:
        copy.wait()


def body(n_p, n_s, snapshots, snap_index, flow_state, eddy_viscosity, intersection, counts):
    start = flow_state[0]
    comps, cells, span, axial = start.shape
    halves = axial // LANES
    us = -(-6 * halves // n_p)
    units = us * n_p
    low_face = lax.ppermute(
        start[:, cells - 1], "pitch", [(i, (i + 1) % n_p) for i in range(n_p)]
    )
    mean, part = stresses(snapshots, snap_index, units)
    blocks = span // BLOCK
    f32 = jnp.float32
    pad = (comps, cells + 2, span + 16, axial)
    smem = pl.BlockSpec(memory_space=pltpu.SMEM)
    vmem = pl.BlockSpec(memory_space=pltpu.VMEM)
    hbm = pl.BlockSpec(memory_space=pl.ANY)
    dma = pltpu.SemaphoreType.DMA
    received, new = pl.pallas_call(
        functools.partial(couple_kernel, n_p, n_s, 1.0 / (SNAPS * cells * n_p)),
        out_shape=(
            jax.ShapeDtypeStruct((6, span, axial), f32),
            jax.ShapeDtypeStruct(start.shape, f32),
        ),
        in_specs=[smem, smem, vmem, hbm, hbm, hbm, hbm],
        out_specs=(vmem, hbm),
        scratch_shapes=[
            pltpu.VMEM((n_p, us, span, LANES), f32),
            pltpu.VMEM((us, blocks, BLOCK, LANES), f32),
            pltpu.VMEM((n_s, CAPACITY, us, BLOCK, LANES), f32),
            pltpu.VMEM((n_s, CAPACITY, us, BLOCK, LANES), f32),
            pltpu.VMEM((units, span, LANES), f32),
            pltpu.VMEM(pad, f32),
            pltpu.VMEM(pad, f32),
            pltpu.VMEM((3, cells, span, axial), f32),
            pltpu.VMEM((cells, span, axial), f32),
            pltpu.VMEM((span, axial), f32),
            pltpu.VMEM((3, span, axial), f32),
            pltpu.VMEM((2, 2, comps, cells, axial), f32),
            pltpu.VMEM((2, 2, comps, cells, axial), f32),
            dma((n_p,)), dma((n_p,)), dma((n_s,)), dma((n_s,)), dma((n_p,)), dma((n_p,)),
            dma((3,)), dma((3,)), dma((2, 2)), dma((2, 2)), dma((4,)), dma((3,)),
        ],
        compiler_params=pltpu.CompilerParams(
            collective_id=0, has_side_effects=True, vmem_limit_bytes=40 * 1024 * 1024
        ),
    )(intersection[0], counts[0], part, low_face, start, mean, eddy_viscosity[0])
    return (received[None], new[None])


def solution(mesh):
    return jax.shard_map(
        functools.partial(body, mesh.shape["pitch"], mesh.shape["span"]),
        mesh=mesh,
        in_specs=(
            P("row", None, None, "pitch", "span", None),
            P(),
            P("row", None, "pitch", "span", None),
            P("row", "pitch", "span", None),
            P("row", None),
            P("row", None),
        ),
        out_specs=(P("row", None, "span", None), P("row", None, "pitch", "span", None)),
        check_vma=False,
    )
```

time: 291 us -> 61.4 us (0.21)
  other arithmetic: 77.3 us -> 0 us
  loops' own time: 63.3 us -> 0 us
  waiting for transfers between devices: 59.3 us -> 0.01 us
  Pallas kernels: 0 us -> 51 us
  local copies, waits for them, and re-layouts: 49.7 us -> 6.38 us
  starting transfers between devices: 22.9 us -> 3.02 us
  between operations: 14.3 us -> 0.7 us
    another operation x2 -> x0, loops' own time: 63.3 us -> none  [the longest x1 32.4 us: body(): lax.fori_loop(0, SNAPS, add_products, jnp.zeros((6, span_cells, axial_cel...]
    pallas_call x0 -> x2, Pallas kernels: none -> 51 us  [the longest x1 40.3 us: body(): pl.pallas_call(functools.partial(couple_kernel, n_p, n_s, 1.0 / (SNAPS *...]
    psum x1 -> x0, waiting for transfers between devices: 44.2 us -> none  [body(): totals = lax.psum(partial_value, 'pitch')]
    dynamic_slice x34 -> x0, local copies, waits for them, and re-layouts: 29.8 us -> none  [the longest x16 20.2 us: add_mean(): return running + select_slot(snap_index[step_num])]
    add x33 -> x0, other arithmetic: 28.6 us -> none  [the longest x16 26.5 us: add_mean(): return running + select_slot(snap_index[step_num])]
    sub x18 -> x0, other arithmetic: 21.9 us -> none  [the longest x16 21.6 us: add_products(): fluct = select_slot(snap_index[step_num]) - time_mean]
    ppermute x9 -> x1, starting transfers between devices: 18.2 us -> 3.02 us  [body(): lax.ppermute(start[:, cells - 1], 'pitch', [(i, (i + 1) % n_p) for i in r...]
    slice x11 -> x0, local copies, waits for them, and re-layouts: 14.7 us -> none  [the longest x4 5.44 us: padded_2(): lax.slice_in_dim(block, 0, width, axis=dim)]
  transfers between devices with their start and end apart: 11 -> 1, of which waited for: 4 -> 0; matrix products, arithmetic and copies ran while one was open for 35% -> 0% of each run, Pallas kernels for 0% -> 18%
where the time goes in v1:
time: 61.4 us; the launch traced here: 61.1 us
  Pallas kernels  51 us (83%)
  local copies, waits for them, and re-layouts  6.38 us (10%)
  starting transfers between devices  3.02 us (5%)
  between operations  0.7 us (1%)
    pallas_call x1, Pallas kernels, body(): pl.pallas_call(functools.partial(couple_kernel, n_p, n_s, 1.0 / (SNAPS *...  40.3 us
    pallas_call x1, Pallas kernels, stresses(): pl.pallas_call(stress_kernel, out_shape=(jax.ShapeDtypeStruct((comps, pit...  10.7 us
    unnamed x14, local copies, waits for them, and re-layouts  4.65 us
    ppermute x1, starting transfers between devices, body(): lax.ppermute(start[:, cells - 1], 'pitch', [(i, (i + 1) % n_p) for i in r...  3.02 us
    squeeze x1, local copies, waits for them, and re-layouts, body(): start[:, cells - 1]  1.73 us
  transfers between devices with their start and end apart: 1, of which 0 were waited for; matrix products, arithmetic and copies ran while one was open for 0% of the time, Pallas kernels for 18%

profile of v1, /device:TPU:0, one launch (start us, length us, event | category | flops | bytes accessed | tf_op | source)
XLA Modules:
  0.0 61.1 jit_solution(11919640450944926172)
XLA Ops:
  0.6 1.7 %slice_bitcast_fusion = f32[5,64,256]{2,1,0:T(8,128)} fusion(f32[5,8,64,256]{3,2,1,0:T(8,128)} %bitcast.8), kind=kLoop, calls=%fused_computation | loop fusion | bytes 655360 | tf_op jit(solution)/shard_map/squeeze | solution.py:364
  2.4 0.0 copy-start
  2.4 0.0 copy-start.2
  2.4 0.0 copy-start.4
  2.4 0.0 copy-start.5
  2.4 3.0 %collective-permute-start = (f32[5,64,256]{2,1,0:T(8,128)}, f32[5,64,256]{2,1,0:T(8,128)S(1)}, u32[]{:S(2)}, u32[]{:S(2)}) collective-permute-start(f32[5,64,256]{2,1,0:T(8,128)} %slice_bitcast_fusion), channel_id=1, source_target_pairs={{0,4},{4,8},{8,12},{12,0},{1,5},{5,9},{9,13},{13,1},{2,6},{6,10},{... | collective-permute-start | bytes 983048 | tf_op jit(solution)/shard_map/ppermute | solution.py:363
  5.4 10.7 %shard_map.77 = (f32[3,8,64,256]{3,2,1,0:T(8,128)}, f32[12,64,128]{2,1,0:T(8,128)}) custom-call(s32[16]{0:T(128)} %refs_0_.1, bf16[1,20,3,8,64,256]{5,4,3,2,1,0:T(8,128)(2,1)} %refs_16_.1, bf16[1,20,3,8,64,256]{5,4,3,2,1,0:T(8,128)(2,1)} %refs_16_.1, bf16[1,20,3,8,64,256]{5,4,3,2,1,0:T(8,128)(2,1)} %refs_16_.1, bf16[1,20,3,8,64,256]{5,4,3,2,1,0:T(8,128)(2,1)} %refs_16_.1, ...), custom_call_target="tpu_custom_call" | custom-call | flops 41943040 | bytes 12582912 | tf_op jit(solution)/shard_map/pallas_call | solution.py:63
  16.1 0.0 collective-permute-done.low_face
  16.1 0.0 copy-done
  16.2 0.0 copy-done.2
  16.2 0.0 copy-done.4
  16.2 0.0 copy-done.5
  16.2 0.0 copy-start.1
  16.2 1.4 %copy-done.1 = f32[3,8,64,256]{3,2,1,0:T(8,128)S(1)} copy-done((f32[3,8,64,256]{3,2,1,0:T(8,128)S(1)}, f32[3,8,64,256]{3,2,1,0:T(8,128)}, u32[]{:S(2)}) %copy-start.1) | copy-done | bytes 1572888
  17.6 0.0 copy-start.3
  17.6 1.0 %copy-done.3 = f32[12,64,128]{2,1,0:T(8,128)S(1)} copy-done((f32[12,64,128]{2,1,0:T(8,128)S(1)}, f32[12,64,128]{2,1,0:T(8,128)}, u32[]{:S(2)}) %copy-start.3) | copy-done | bytes 393240
  18.6 40.3 %shard_map.78 = (f32[6,64,256]{2,1,0:T(8,128)S(1)}, f32[5,8,64,256]{3,2,1,0:T(8,128)S(1)}) custom-call(s32[32]{0:T(128)S(1)} %bitcast.13, s32[32]{0:T(128)S(1)} %bitcast.14, f32[12,64,128]{2,1,0:T(8,128)S(1)} %copy-done.3, f32[5,64,256]{2,1,0:T(8,128)S(1)} %collective-permute-done.low_face, f32[5,8,64,256]{3,2,1,0:T(8,128)S(1)} %bitcast.9, ...), custom_call_target="tpu_custom_call" | custom-call | tf_op jit(solution)/shard_map/pallas_call | solution.py:374
  58.9 0.7 %copy.10 = f32[1,6,64,256]{3,2,1,0:T(8,128)} copy(f32[1,6,64,256]{3,2,1,0:T(8,128)S(1)} %bitcast.12) | data formatting | bytes 786432
  59.7 1.5 %copy.11 = f32[1,5,8,64,256]{4,3,2,1,0:T(8,128)} copy(f32[1,5,8,64,256]{4,3,2,1,0:T(8,128)S(1)} %bitcast.10) | data formatting | bytes 5242880
Async XLA Ops:
  2.4 13.8 %copy-start = (f32[1,5,8,64,256]{4,3,2,1,0:T(8,128)S(1)}, f32[1,5,8,64,256]{4,3,2,1,0:T(8,128)}, u32[]{:S(2)}) copy-start(f32[1,5,8,64,256]{4,3,2,1,0:T(8,128)} %param.8) | copy-start | bytes 7864324
  2.4 13.8 %copy-start.2 = (f32[1,8,64,256]{3,2,1,0:T(8,128)S(1)}, f32[1,8,64,256]{3,2,1,0:T(8,128)}, u32[]{:S(2)}) copy-start(f32[1,8,64,256]{3,2,1,0:T(8,128)} %param.9) | copy-start | bytes 1572868
  2.4 13.8 %copy-start.4 = (s32[1,32]{1,0:T(1,128)S(1)}, s32[1,32]{1,0:T(1,128)}, u32[]{:S(2)}) copy-start(s32[1,32]{1,0:T(1,128)} %param.10) | copy-start | bytes 388
  2.4 13.8 %copy-start.5 = (s32[1,32]{1,0:T(1,128)S(1)}, s32[1,32]{1,0:T(1,128)}, u32[]{:S(2)}) copy-start(s32[1,32]{1,0:T(1,128)} %param.11) | copy-start | bytes 388
  2.4 13.8 %collective-permute-start = (f32[5,64,256]{2,1,0:T(8,128)}, f32[5,64,256]{2,1,0:T(8,128)S(1)}, u32[]{:S(2)}, u32[]{:S(2)}) collective-permute-start(f32[5,64,256]{2,1,0:T(8,128)} %slice_bitcast_fusion), channel_id=1, source_target_pairs={{0,4},{4,8},{8,12},{12,0},{1,5},{5,9},{9,13},{13,1},{2,6},{6,10},{... | collective-permute-start | bytes 983048 | tf_op jit(solution)/shard_map/ppermute | solution.py:363
  16.2 1.4 %copy-start.1 = (f32[3,8,64,256]{3,2,1,0:T(8,128)S(1)}, f32[3,8,64,256]{3,2,1,0:T(8,128)}, u32[]{:S(2)}) copy-start(f32[3,8,64,256]{3,2,1,0:T(8,128)} %get-tuple-element.7.mean_hbm) | copy-start | bytes 4718596
  17.6 1.0 %copy-start.3 = (f32[12,64,128]{2,1,0:T(8,128)S(1)}, f32[12,64,128]{2,1,0:T(8,128)}, u32[]{:S(2)}) copy-start(f32[12,64,128]{2,1,0:T(8,128)} %get-tuple-element.6.part) | copy-start | bytes 1179652

commit v2 on v1

--- a/solution.py
+++ b/solution.py
@@ -18,16 +18,15 @@
 time_step = 0.1
 
 
-def stress_kernel(*refs):
-    snaps, (mean_ref, part_ref) = refs[1 : 1 + SNAPS], refs[1 + SNAPS :]
-    cells = mean_ref.shape[1]
-    halves = mean_ref.shape[3] // LANES
+def stress_tile(snaps, slots, mean, part, rows):
+    cells = mean.shape[1]
+    halves = mean.shape[3] // LANES
     for h in range(halves):
         cols = slice(h * LANES, (h + 1) * LANES)
 
         def one(i, acc):
             def load(t):
-                return [snaps[t][0, 0, c, i, :, cols].astype(jnp.float32) for c in range(3)]
+                return [snaps[slots[t], c, i, :, cols].astype(jnp.float32) for c in range(3)]
 
             base = load(0)
             sums, prods = None, None
@@ -39,7 +38,7 @@
                 prods = pr if prods is None else [a + b for a, b in zip(prods, pr)]
             shift = [s * (1.0 / SNAPS) for s in sums]
             for c in range(3):
-                mean_ref[c, i, :, cols] = base[c] + shift[c]
+                mean[c, i, rows, cols] = base[c] + shift[c]
             return tuple(
                 a + (pr - sums[p] * shift[q]) for a, pr, (p, q) in zip(acc, prods, stress_pairs)
             )
@@ -47,40 +46,9 @@
         zero = jnp.zeros((ROWS_BF16, LANES), jnp.float32)
         acc = lax.fori_loop(0, cells, one, (zero,) * 6)
         for m in range(6):
-            part_ref[m * halves + h] = acc[m]
-    for u in range(6 * halves, part_ref.shape[0]):
-        part_ref[u] = jnp.zeros((ROWS_BF16, LANES), jnp.float32)
-
-
-def stresses(snapshots, snap_index, units):
-    _, _, comps, pitch, span, axial = snapshots.shape
-
-    def spec(t):
-        return pl.BlockSpec(
-            (1, 1, comps, pitch, ROWS_BF16, axial), lambda j, idx: (0, idx[t], 0, 0, j, 0)
-        )
-
-    return pl.pallas_call(
-        stress_kernel,
-        out_shape=(
-            jax.ShapeDtypeStruct((comps, pitch, span, axial), jnp.float32),
-            jax.ShapeDtypeStruct((units, span, LANES), jnp.float32),
-        ),
-        grid_spec=pltpu.PrefetchScalarGridSpec(
-            num_scalar_prefetch=1,
-            grid=(span // ROWS_BF16,),
-            in_specs=[spec(t) for t in range(SNAPS)],
-            out_specs=(
-                pl.BlockSpec((comps, pitch, ROWS_BF16, axial), lambda j, idx: (0, 0, j, 0)),
-                pl.BlockSpec((units, ROWS_BF16, LANES), lambda j, idx: (0, j, 0)),
-            ),
-        ),
-        cost_estimate=pl.CostEstimate(
-            flops=SNAPS * 20 * pitch * span * axial,
-            bytes_accessed=SNAPS * comps * pitch * span * axial * 2,
-            transcendentals=0,
-        ),
-    )(snap_index, *([snapshots] * SNAPS))
+            part[m * halves + h, rows] = acc[m]
+    for u in range(6 * halves, part.shape[0]):
+        part[u, rows] = jnp.zeros((ROWS_BF16, LANES), jnp.float32)
 
 
 def next_cell(x):
@@ -95,30 +63,38 @@
 
 def couple_kernel(
     n_p, n_s, scale,
-    links, counts, part, low_face, q_hbm, mean_hbm, visc_hbm,
+    slot_list, links, counts, snaps_hbm, q_hbm, visc_hbm,
     rec_out, new_hbm,
-    rs_buf, tot, out_buf, a2a, rec, qpad, spad, mean, visc, dtm, src,
+    snaps_even, snaps_odd, part, rs_buf, tot, out_buf, a2a, rec, qpad, spad, mean, visc, dtm, src,
     zsend, zrecv,
-    rs_s, rs_r, aa_s, aa_r, ag_s, ag_r, hp_s, hp_r, hz_s, hz_r, loc, out_sem,
+    rs_s, rs_r, aa_s, aa_r, ag_s, ag_r, hp_s, hp_r, hz_s, hz_r, loc, snap_sem, out_sem,
 ):
     r, p, s = lax.axis_index("row"), lax.axis_index("pitch"), lax.axis_index("span")
     comps, cells, span, axial = q_hbm.shape
     us = part.shape[0] // n_p
     blocks = span // BLOCK
     halves = axial // LANES
-    tile = 16
+    tile = ROWS_BF16
     top = 8
 
+    tiles = span // tile
+
+    snaps = (snaps_even, snaps_odd)
+
+    def load_snaps(j):
+        return pltpu.make_async_copy(
+            snaps_hbm.at[:, :, :, pl.ds(j * tile, tile)], snaps[j % 2], snap_sem.at[j]
+        )
+
+    loads = [load_snaps(j) for j in range(tiles)]
+    loads[0].start()
     load_q = pltpu.make_async_copy(
         q_hbm, qpad.at[:, pl.ds(1, cells), pl.ds(top, span)], loc.at[0]
     )
     load_q.start()
-    load_low = pltpu.make_async_copy(low_face, qpad.at[:, 0, pl.ds(top, span)], loc.at[1])
-    load_low.start()
-    load_mean = pltpu.make_async_copy(mean_hbm, mean, loc.at[2])
-    load_mean.start()
-    load_visc = pltpu.make_async_copy(visc_hbm, visc, loc.at[3])
+    load_visc = pltpu.make_async_copy(visc_hbm, visc, loc.at[1])
     load_visc.start()
+    loads[1].start()
 
     barrier = pltpu.get_barrier_semaphore()
     for d in range(n_p):
@@ -131,16 +107,6 @@
         pl.semaphore_signal(barrier, inc=1, device_id=(r, p, to), device_id_type=MESH)
     pl.semaphore_wait(barrier, 2 * n_p + n_s - 2)
 
-    scatter = []
-    for d in range(n_p):
-        to = lax.rem(p + d, n_p)
-        scatter.append(pltpu.make_async_remote_copy(
-            src_ref=part.at[pl.ds(to * us, us)], dst_ref=rs_buf.at[d],
-            send_sem=rs_s.at[d], recv_sem=rs_r.at[d],
-            device_id=(1 - r, to, s), device_id_type=MESH,
-        ))
-    for copy in scatter:
-        copy.start()
     right, left = lax.rem(p + 1, n_p), lax.rem(p + n_p - 1, n_p)
     above, below = lax.rem(s + 1, n_s), lax.rem(s + n_s - 1, n_s)
     high_q = pltpu.make_async_remote_copy(
@@ -148,7 +114,12 @@
         send_sem=hp_s.at[0], recv_sem=hp_r.at[0],
         device_id=(r, left, s), device_id_type=MESH,
     )
-    high_q.start()
+    low_q = pltpu.make_async_remote_copy(
+        src_ref=q_hbm.at[:, cells - 1], dst_ref=qpad.at[:, 0, pl.ds(top, span)],
+        send_sem=hp_s.at[3], recv_sem=hp_r.at[3],
+        device_id=(r, right, s), device_id_type=MESH,
+    )
+    low_q.start()
 
     def span_faces(pad, k):
         def pack(i, carry):
@@ -183,8 +154,26 @@
         lax.fori_loop(0, cells, land, 0)
 
     load_q.wait()
-    load_low.wait()
     q_span = span_faces(qpad, 0)
+
+    slots = [slot_list[t] for t in range(SNAPS)]
+    scatter = []
+    for j in range(tiles):
+        loads[j].wait()
+        stress_tile(snaps[j % 2], slots, mean, part, slice(j * tile, (j + 1) * tile))
+        if j + 2 < tiles:
+            loads[j + 2].start()
+        for d in range(n_p):
+            to = lax.rem(p + d, n_p)
+            copy = pltpu.make_async_remote_copy(
+                src_ref=part.at[pl.ds(to * us, us), pl.ds(j * tile, tile)],
+                dst_ref=rs_buf.at[d, :, pl.ds(j * tile, tile)],
+                send_sem=rs_s.at[d, j], recv_sem=rs_r.at[d, j],
+                device_id=(1 - r, to, s), device_id_type=MESH,
+            )
+            copy.start()
+            scatter.append(copy)
+    high_q.start()
 
     for j in range(span // tile):
         row = lax.broadcasted_iota(jnp.int32, (tile, axial), 0)
@@ -253,8 +242,8 @@
     for copy in q_span:
         copy.wait()
     span_land(qpad, 0)
-    load_mean.wait()
     load_visc.wait()
+    low_q.wait()
     high_q.wait()
     for copy in gather:
         copy.wait()
@@ -360,16 +349,13 @@
     halves = axial // LANES
     us = -(-6 * halves // n_p)
     units = us * n_p
-    low_face = lax.ppermute(
-        start[:, cells - 1], "pitch", [(i, (i + 1) % n_p) for i in range(n_p)]
-    )
-    mean, part = stresses(snapshots, snap_index, units)
     blocks = span // BLOCK
+    tiles = span // ROWS_BF16
     f32 = jnp.float32
     pad = (comps, cells + 2, span + 16, axial)
     smem = pl.BlockSpec(memory_space=pltpu.SMEM)
     vmem = pl.BlockSpec(memory_space=pltpu.VMEM)
-    hbm = pl.BlockSpec(memory_space=pl.ANY)
+    hbm = pl.BlockSpec(memory_space=pltpu.HBM)
     dma = pltpu.SemaphoreType.DMA
     received, new = pl.pallas_call(
         functools.partial(couple_kernel, n_p, n_s, 1.0 / (SNAPS * cells * n_p)),
@@ -377,9 +363,12 @@
             jax.ShapeDtypeStruct((6, span, axial), f32),
             jax.ShapeDtypeStruct(start.shape, f32),
         ),
-        in_specs=[smem, smem, vmem, hbm, hbm, hbm, hbm],
-        out_specs=(vmem, hbm),
+        in_specs=[smem, smem, smem, hbm, hbm, hbm],
+        out_specs=(vmem, pl.BlockSpec(memory_space=pl.ANY)),
         scratch_shapes=[
+            pltpu.VMEM((snapshots.shape[1], 3, cells, ROWS_BF16, axial), snapshots.dtype),
+            pltpu.VMEM((snapshots.shape[1], 3, cells, ROWS_BF16, axial), snapshots.dtype),
+            pltpu.VMEM((units, span, LANES), f32),
             pltpu.VMEM((n_p, us, span, LANES), f32),
             pltpu.VMEM((us, blocks, BLOCK, LANES), f32),
             pltpu.VMEM((n_s, CAPACITY, us, BLOCK, LANES), f32),
@@ -393,13 +382,14 @@
             pltpu.VMEM((3, span, axial), f32),
             pltpu.VMEM((2, 2, comps, cells, axial), f32),
             pltpu.VMEM((2, 2, comps, cells, axial), f32),
-            dma((n_p,)), dma((n_p,)), dma((n_s,)), dma((n_s,)), dma((n_p,)), dma((n_p,)),
-            dma((3,)), dma((3,)), dma((2, 2)), dma((2, 2)), dma((4,)), dma((3,)),
+            dma((n_p, tiles)), dma((n_p, tiles)),
+            dma((n_s,)), dma((n_s,)), dma((n_p,)), dma((n_p,)),
+            dma((4,)), dma((4,)), dma((2, 2)), dma((2, 2)), dma((2,)), dma((tiles,)), dma((3,)),
         ],
         compiler_params=pltpu.CompilerParams(
             collective_id=0, has_side_effects=True, vmem_limit_bytes=40 * 1024 * 1024
         ),
-    )(intersection[0], counts[0], part, low_face, start, mean, eddy_viscosity[0])
+    )(snap_index, intersection[0], counts[0], snapshots[0], start, eddy_viscosity[0])
     return (received[None], new[None])
 
 

time: 61.4 us -> 56.2 us (0.915)
  starting transfers between devices: 3.02 us -> 0 us
  Pallas kernels: 51 us -> 48.3 us
    pallas_call x1 -> x0, Pallas kernels: 10.7 us -> none  [stresses(): pl.pallas_call(stress_kernel, out_shape=(jax.ShapeDtypeStruct((comps, pit...]
    pallas_call x1, Pallas kernels: 40.3 us -> 48.3 us  [body(): pl.pallas_call(functools.partial(couple_kernel, n_p, n_s, 1.0 / (SNAPS *...]
    ppermute x1 -> x0, starting transfers between devices: 3.02 us -> none  [body(): lax.ppermute(start[:, cells - 1], 'pitch', [(i, (i + 1) % n_p) for i in r...]
    unnamed x14 -> x12, local copies, waits for them, and re-layouts: 4.65 us -> 6.98 us
    squeeze x1 -> x0, local copies, waits for them, and re-layouts: 1.73 us -> none  [body(): start[:, cells - 1]]
  transfers between devices with their start and end apart: 1 -> 0, of which waited for: 0 -> 0; matrix products, arithmetic and copies ran while one was open for 0% -> 0% of each run, Pallas kernels for 18% -> 0%
where the time goes in v2:
time: 56.2 us; the launch traced here: 55.9 us
  Pallas kernels  48.3 us (86%)
  local copies, waits for them, and re-layouts  6.98 us (12%)
  between operations  0.65 us (1%)
    pallas_call x1, Pallas kernels, body(): pl.pallas_call(functools.partial(couple_kernel, n_p, n_s, 1.0 / (SNAPS *...  48.3 us
    unnamed x12, local copies, waits for them, and re-layouts  6.98 us

profile of v2, /device:TPU:0, one launch (start us, length us, event | category | flops | bytes accessed | tf_op | source)
XLA Modules:
  0.0 55.9 jit_solution(13873702607239827090)
XLA Ops:
  0.6 0.0 copy-start
  0.6 1.7 %copy-done = f32[1,5,8,64,256]{4,3,2,1,0:T(8,128)S(1)} copy-done((f32[1,5,8,64,256]{4,3,2,1,0:T(8,128)S(1)}, f32[1,5,8,64,256]{4,3,2,1,0:T(8,128)}, u32[]{:S(2)}) %copy-start) | copy-done | bytes 2621464
  2.4 0.0 copy-start.1
  2.4 1.0 %copy-done.1 = f32[1,8,64,256]{3,2,1,0:T(8,128)S(1)} copy-done((f32[1,8,64,256]{3,2,1,0:T(8,128)S(1)}, f32[1,8,64,256]{3,2,1,0:T(8,128)}, u32[]{:S(2)}) %copy-start.1) | copy-done | bytes 524312
  3.4 0.0 copy-start.2
  3.4 0.7 %copy-done.2 = s32[16]{0:T(128)S(1)} copy-done((s32[16]{0:T(128)S(1)}, s32[16]{0:T(128)}, u32[]{:S(2)}) %copy-start.2) | copy-done | bytes 88
  4.1 0.0 copy-start.3
  4.1 0.7 %copy-done.3 = s32[1,32]{1,0:T(1,128)S(1)} copy-done((s32[1,32]{1,0:T(1,128)S(1)}, s32[1,32]{1,0:T(1,128)}, u32[]{:S(2)}) %copy-start.3) | copy-done | bytes 152
  4.7 0.0 copy-start.4
  4.7 0.7 %copy-done.4 = s32[1,32]{1,0:T(1,128)S(1)} copy-done((s32[1,32]{1,0:T(1,128)S(1)}, s32[1,32]{1,0:T(1,128)}, u32[]{:S(2)}) %copy-start.4) | copy-done | bytes 152
  5.4 48.3 %shard_map.77 = (f32[6,64,256]{2,1,0:T(8,128)S(1)}, f32[5,8,64,256]{3,2,1,0:T(8,128)S(1)}) custom-call(s32[16]{0:T(128)S(1)} %copy-done.2, s32[32]{0:T(128)S(1)} %bitcast.11, s32[32]{0:T(128)S(1)} %bitcast.12, bf16[20,3,8,64,256]{4,3,2,1,0:T(8,128)(2,1)} %bitcast.13, f32[5,8,64,256]{3,2,1,0:T(8,128)S(1)} %bitcast.8, f32[8,64,256]{2,1,0:T(8,128)S(1)} %bitcast.9), custom_call_target="tpu_custom_call" | custom-call | tf_op jit(solution)/shard_map/pallas_call | solution.py:360
  53.7 0.7 %copy.10 = f32[1,6,64,256]{3,2,1,0:T(8,128)} copy(f32[1,6,64,256]{3,2,1,0:T(8,128)S(1)} %bitcast.10) | data formatting | bytes 786432
  54.4 1.5 %copy.11 = f32[1,5,8,64,256]{4,3,2,1,0:T(8,128)} copy(f32[1,5,8,64,256]{4,3,2,1,0:T(8,128)S(1)} %bitcast.7) | data formatting | bytes 5242880
Async XLA Ops:
  0.6 1.7 %copy-start = (f32[1,5,8,64,256]{4,3,2,1,0:T(8,128)S(1)}, f32[1,5,8,64,256]{4,3,2,1,0:T(8,128)}, u32[]{:S(2)}) copy-start(f32[1,5,8,64,256]{4,3,2,1,0:T(8,128)} %param.8) | copy-start | bytes 7864324
  2.4 1.0 %copy-start.1 = (f32[1,8,64,256]{3,2,1,0:T(8,128)S(1)}, f32[1,8,64,256]{3,2,1,0:T(8,128)}, u32[]{:S(2)}) copy-start(f32[1,8,64,256]{3,2,1,0:T(8,128)} %param.9) | copy-start | bytes 1572868
  3.4 0.7 %copy-start.2 = (s32[16]{0:T(128)S(1)}, s32[16]{0:T(128)}, u32[]{:S(2)}) copy-start(s32[16]{0:T(128)} %slot_list.1) | copy-start | bytes 196
  4.1 0.7 %copy-start.3 = (s32[1,32]{1,0:T(1,128)S(1)}, s32[1,32]{1,0:T(1,128)}, u32[]{:S(2)}) copy-start(s32[1,32]{1,0:T(1,128)} %param.10) | copy-start | bytes 388
  4.7 0.7 %copy-start.4 = (s32[1,32]{1,0:T(1,128)S(1)}, s32[1,32]{1,0:T(1,128)}, u32[]{:S(2)}) copy-start(s32[1,32]{1,0:T(1,128)} %param.11) | copy-start | bytes 388

commit v3 on v2

--- a/solution.py
+++ b/solution.py
@@ -265,8 +265,8 @@
         src[2, rows] = live * (-diff[2] - 2.0 * curve * t[4])
 
     def section(pad, i, finish):
-        for j in range(span // tile):
-            rows = slice(j * tile, (j + 1) * tile)
+        for j in range(span // BLOCK):
+            rows = slice(j * BLOCK, (j + 1) * BLOCK)
             nu = visc[i, rows]
             means = [mean[c, i, rows] for c in range(3)]
             speed = 0.5 + means[0]
@@ -277,24 +277,27 @@
             force = [src[c, rows] for c in range(3)]
             energy = means[0] * force[0] + means[1] * force[1] + means[2] * force[2]
             force = [None] + force + [energy]
-            at = top + j * tile
+            steps = []
+            at = top + j * BLOCK
             for c in range(comps):
-                x = pad[c, i + 1, at : at + tile]
+                x = pad[c, i + 1, at : at + BLOCK]
                 around = (
-                    pad[c, i, at : at + tile] + pad[c, i + 2, at : at + tile]
-                    + pad[c, i + 1, at - 1 : at + tile - 1]
-                    + pad[c, i + 1, at + 1 : at + tile + 1]
+                    pad[c, i, at : at + BLOCK] + pad[c, i + 2, at : at + BLOCK]
+                    + pad[c, i + 1, at - 1 : at + BLOCK - 1]
+                    + pad[c, i + 1, at + 1 : at + BLOCK + 1]
                 )
                 step = (
                     ahead * next_cell(x) + behind * last_cell(x) + nu * (around - 6.0 * x)
                 )
                 if force[c] is not None:
                     step = step + force[c]
-                finish(c, i, at, x, step)
+                steps.append((x, step))
+            finish(i, at, steps)
 
     def first(i, carry):
-        def finish(c, i, at, x, step):
-            spad[c, i + 1, at : at + tile] = x + step
+        def finish(i, at, steps):
+            for c, (x, step) in enumerate(steps):
+                spad[c, i + 1, at : at + BLOCK] = x + step
 
         section(qpad, i, finish)
         return carry
@@ -302,9 +305,13 @@
     outs = []
 
     def second(i, carry):
-        def finish(c, i, at, x, step):
-            old = qpad[c, i + 1, at : at + tile]
-            qpad[c, i + 1, at : at + tile] = 0.5 * (old + x + step)
+        def finish(i, at, steps):
+            ends = [
+                0.5 * (qpad[c, i + 1, at : at + BLOCK] + x + step)
+                for c, (x, step) in enumerate(steps)
+            ]
+            for c, end in enumerate(ends):
+                qpad[c, i + 1, at : at + BLOCK] = end
 
         section(spad, i, finish)
         return carry

time: 56.2 us -> 56.2 us (level)
  no operation moved by 1% of the time
where the time goes in v3:
time: 56.2 us; the launch traced here: 55.9 us
  Pallas kernels  48.3 us (86%)
  local copies, waits for them, and re-layouts  6.98 us (12%)
  between operations  0.65 us (1%)
    pallas_call x1, Pallas kernels, body(): pl.pallas_call(functools.partial(couple_kernel, n_p, n_s, 1.0 / (SNAPS *...  48.3 us
    unnamed x12, local copies, waits for them, and re-layouts  6.98 us

profile of v3, /device:TPU:0, one launch (start us, length us, event | category | flops | bytes accessed | tf_op | source)
XLA Modules:
  0.0 55.9 jit_solution(9192752378256359546)
XLA Ops:
  0.6 0.0 copy-start
  0.6 1.7 %copy-done = f32[1,5,8,64,256]{4,3,2,1,0:T(8,128)S(1)} copy-done((f32[1,5,8,64,256]{4,3,2,1,0:T(8,128)S(1)}, f32[1,5,8,64,256]{4,3,2,1,0:T(8,128)}, u32[]{:S(2)}) %copy-start) | copy-done | bytes 2621464
  2.4 0.0 copy-start.1
  2.4 1.0 %copy-done.1 = f32[1,8,64,256]{3,2,1,0:T(8,128)S(1)} copy-done((f32[1,8,64,256]{3,2,1,0:T(8,128)S(1)}, f32[1,8,64,256]{3,2,1,0:T(8,128)}, u32[]{:S(2)}) %copy-start.1) | copy-done | bytes 524312
  3.4 0.0 copy-start.2
  3.4 0.7 %copy-done.2 = s32[16]{0:T(128)S(1)} copy-done((s32[16]{0:T(128)S(1)}, s32[16]{0:T(128)}, u32[]{:S(2)}) %copy-start.2) | copy-done | bytes 88
  4.1 0.0 copy-start.3
  4.1 0.7 %copy-done.3 = s32[1,32]{1,0:T(1,128)S(1)} copy-done((s32[1,32]{1,0:T(1,128)S(1)}, s32[1,32]{1,0:T(1,128)}, u32[]{:S(2)}) %copy-start.3) | copy-done | bytes 152
  4.7 0.0 copy-start.4
  4.7 0.7 %copy-done.4 = s32[1,32]{1,0:T(1,128)S(1)} copy-done((s32[1,32]{1,0:T(1,128)S(1)}, s32[1,32]{1,0:T(1,128)}, u32[]{:S(2)}) %copy-start.4) | copy-done | bytes 152
  5.4 48.3 %shard_map.77 = (f32[6,64,256]{2,1,0:T(8,128)S(1)}, f32[5,8,64,256]{3,2,1,0:T(8,128)S(1)}) custom-call(s32[16]{0:T(128)S(1)} %copy-done.2, s32[32]{0:T(128)S(1)} %bitcast.11, s32[32]{0:T(128)S(1)} %bitcast.12, bf16[20,3,8,64,256]{4,3,2,1,0:T(8,128)(2,1)} %bitcast.13, f32[5,8,64,256]{3,2,1,0:T(8,128)S(1)} %bitcast.8, f32[8,64,256]{2,1,0:T(8,128)S(1)} %bitcast.9), custom_call_target="tpu_custom_call" | custom-call | tf_op jit(solution)/shard_map/pallas_call | solution.py:367
  53.6 0.7 %copy.10 = f32[1,6,64,256]{3,2,1,0:T(8,128)} copy(f32[1,6,64,256]{3,2,1,0:T(8,128)S(1)} %bitcast.10) | data formatting | bytes 786432
  54.4 1.5 %copy.11 = f32[1,5,8,64,256]{4,3,2,1,0:T(8,128)} copy(f32[1,5,8,64,256]{4,3,2,1,0:T(8,128)S(1)} %bitcast.7) | data formatting | bytes 5242880
Async XLA Ops:
  0.6 1.7 %copy-start = (f32[1,5,8,64,256]{4,3,2,1,0:T(8,128)S(1)}, f32[1,5,8,64,256]{4,3,2,1,0:T(8,128)}, u32[]{:S(2)}) copy-start(f32[1,5,8,64,256]{4,3,2,1,0:T(8,128)} %param.8) | copy-start | bytes 7864324
  2.4 1.0 %copy-start.1 = (f32[1,8,64,256]{3,2,1,0:T(8,128)S(1)}, f32[1,8,64,256]{3,2,1,0:T(8,128)}, u32[]{:S(2)}) copy-start(f32[1,8,64,256]{3,2,1,0:T(8,128)} %param.9) | copy-start | bytes 1572868
  3.4 0.7 %copy-start.2 = (s32[16]{0:T(128)S(1)}, s32[16]{0:T(128)}, u32[]{:S(2)}) copy-start(s32[16]{0:T(128)} %slot_list.1) | copy-start | bytes 196
  4.1 0.7 %copy-start.3 = (s32[1,32]{1,0:T(1,128)S(1)}, s32[1,32]{1,0:T(1,128)}, u32[]{:S(2)}) copy-start(s32[1,32]{1,0:T(1,128)} %param.10) | copy-start | bytes 388
  4.7 0.7 %copy-start.4 = (s32[1,32]{1,0:T(1,128)S(1)}, s32[1,32]{1,0:T(1,128)}, u32[]{:S(2)}) copy-start(s32[1,32]{1,0:T(1,128)} %param.11) | copy-start | bytes 388
